TPU v7x, 32 devices: a whole 2x2x4 slice. The times are simulated.
32 devices in a mesh: pos: 2 (over x), gz: 16 (over z, y, core).
Axes of the slice: x: 2, y: 2, z: 4, core: 2. Of those that a mesh axis runs over, the one named last changes fastest.
Arguments:
- source: float32 [16, 512, 256], P('gz', 'pos'), parts along dimension 1
- regions: int32 [16, 512, 256], P('gz', 'pos'), parts along dimension 1, may hold values from 0 to 3
- reluctivity: float32 [4], replicated, may hold values from 0.25 to 2
- levels: float32 [4], replicated, may hold values from 0.5 to 1.5
- seeds: int32 [4, 4], replicated, may hold values from 0 to 3, as said below
- band_cells: int32 [4096], P('pos'), parts along dimension 0, may hold values from 0 to 65535, as said below
- sector_order: int32 [4096], P('pos'), parts along dimension 0, may hold values from 0 to 2047, each once
Outputs:
- solution: float32 [4, 16, 512, 256], P(None, 'gz', 'pos'), parts along dimension 2
- forces: float32 [2, 8, 32, 16], P(None, 'pos', 'gz'), parts along dimension 1
There are 2 independent parts, one for each index of `pos`. A program takes and returns all parts, laid end to end along the dimension named above; an argument that names none is the same for every part. Nothing has to cross between parts.
Inputs may be any that keep to these rules, and one draw needn't show every extreme that they name: `seeds`: every level is named by exactly 4 entries. `band_cells`: distinct cells. `sector_order`: each band entry once.
All inputs are finite; a program needn't handle non-finite values.
Results may differ from a plain program's by a relative error of at most 0.0003.
Values sent between devices are 32-bit elements; how exact they have to be, the bound alone decides.
No kernel may reach another device: no remote copies, remote signals or barrier semaphores. Data moves between devices by JAX's collectives and lax.ppermute only.
A program may use at most 128 MiB of HBM per device.

v0:
```python
import jax
import jax.numpy as jnp
from jax import lax
from jax.sharding import PartitionSpec as P

ITERS = 2
PER_SEC = 64
MASS_SHIFT = 0.5


def with_halo(block, sides, width):
    for axis, dim in sides:
        count = lax.axis_size(axis)
        forward = [(i, i + 1) for i in range(count - 1)]
        backward = [(target, source) for source, target in forward]
        low = lax.ppermute(
            lax.slice_in_dim(block, block.shape[dim] - width, None, axis=dim), axis, forward
        )
        high = lax.ppermute(lax.slice_in_dim(block, 0, width, axis=dim), axis, backward)
        block = jnp.concatenate([low, block, high], axis=dim)
    return block


def face_weights(reluct_cell, padded):
    return (
        0.5 * (reluct_cell + padded[:-2, 1:-1, 1:-1]),
        0.5 * (reluct_cell + padded[2:, 1:-1, 1:-1]),
        0.5 * (reluct_cell + padded[1:-1, :-2, 1:-1]),
        0.5 * (reluct_cell + padded[1:-1, 2:, 1:-1]),
        0.5 * (reluct_cell + padded[1:-1, 1:-1, :-2]),
        0.5 * (reluct_cell + padded[1:-1, 1:-1, 2:]),
    )


def apply_stencil(field, padded, weights):
    total = MASS_SHIFT * field
    total = total + weights[0][None] * (field - padded[:, :-2, 1:-1, 1:-1])
    total = total + weights[1][None] * (field - padded[:, 2:, 1:-1, 1:-1])
    total = total + weights[2][None] * (field - padded[:, 1:-1, :-2, 1:-1])
    total = total + weights[3][None] * (field - padded[:, 1:-1, 2:, 1:-1])
    total = total + weights[4][None] * (field - padded[:, 1:-1, 1:-1, :-2])
    total = total + weights[5][None] * (field - padded[:, 1:-1, 1:-1, 2:])
    return total


def operate(field, weights):
    axial = with_halo(field, (("gz", 1),), 1)
    padded = jnp.pad(axial, ((0, 0), (0, 0), (1, 1), (1, 1)))
    return apply_stencil(field, padded, weights)


def band_stress(field, band_cells, sector_order):
    count_cols, depth, width_x, width_y = field.shape
    padded = jnp.pad(field, ((0, 0), (0, 0), (1, 1), (1, 1)))
    flux_x = 0.5 * (padded[:, :, 1:-1, 2:] - padded[:, :, 1:-1, :-2])
    flux_y = -0.5 * (padded[:, :, 2:, 1:-1] - padded[:, :, :-2, 1:-1])
    ordered = jnp.take(band_cells, sector_order)
    picked_x = jnp.take(flux_x.reshape(count_cols, depth, width_x * width_y), ordered, axis=2)
    picked_y = jnp.take(flux_y.reshape(count_cols, depth, width_x * width_y), ordered, axis=2)
    row_index = (ordered // width_y).astype(jnp.float32)
    column_index = (ordered % width_y).astype(jnp.float32)
    normal_x = (row_index - 0.5 * (width_x - 1)) / (0.5 * width_x)
    normal_y = (column_index - 0.5 * (width_y - 1)) / (0.5 * width_y)
    normal_part = picked_x * normal_x + picked_y * normal_y
    half_square = 0.5 * (picked_x * picked_x + picked_y * picked_y)
    force_x = picked_x * normal_part - half_square * normal_x
    force_y = picked_y * normal_part - half_square * normal_y
    return jnp.stack([force_x, force_y])


def column_sum(first, second):
    return jnp.sum(first * second, axis=(1, 2, 3))


def widen(vector):
    return vector[:, None, None, None]


def squares(residual):
    return lax.psum(column_sum(residual, residual), "gz")


def body(source, regions, reluctivity, levels, seeds, band_cells, sector_order):
    count_regions = reluctivity.shape[0]
    count_levels = levels.shape[0]
    count_cols = seeds.shape[0]
    level_pick = (
        seeds[:, :, None] == jnp.arange(count_levels, dtype=jnp.int32)[None, None, :]
    ).astype(jnp.float32)
    strength = jnp.sum(level_pick * levels[None, None, :], axis=2)
    reluct_cell = jnp.zeros(source.shape, jnp.float32)
    scaling = jnp.zeros((count_cols,) + source.shape, jnp.float32)
    for region in range(count_regions):
        member = (regions == region).astype(jnp.float32)
        reluct_cell = reluct_cell + reluctivity[region] * member
        scaling = scaling + widen(strength[:, region]) * member[None]
    right_side = scaling * source[None]
    axial_reluct = with_halo(reluct_cell, (("gz", 0),), 1)
    weights = face_weights(reluct_cell, jnp.pad(axial_reluct, ((0, 0), (1, 1), (1, 1))))
    solution = jnp.zeros_like(right_side)
    residual = right_side
    direction = right_side
    norm_now = squares(residual)
    for iteration in range(ITERS):
        image = operate(direction, weights)
        curvature = lax.psum(column_sum(direction, image), "gz")
        step_size = norm_now / curvature
        solution = solution + widen(step_size) * direction
        residual = residual - widen(step_size) * image
        if iteration + 1 < ITERS:
            norm_next = squares(residual)
            direction = residual + widen(norm_next / norm_now) * direction
            norm_now = norm_next
    stress = band_stress(solution, band_cells, sector_order)
    depth = stress.shape[2]
    band_total = stress.shape[3]
    cell_forces = stress.reshape(2 * count_cols, depth, band_total // PER_SEC, PER_SEC)
    sector_sums = jnp.sum(cell_forces, axis=-1)
    gathered = lax.all_to_all(sector_sums, "gz", split_axis=2, concat_axis=1, tiled=True)
    full_depth = gathered.shape[1]
    local_sectors = gathered.shape[2]
    return (
        solution,
        gathered.reshape(2, count_cols, full_depth, local_sectors).transpose(0, 1, 3, 2),
    )


def solution(mesh):
    in_specs = (P("gz", "pos", None), P("gz", "pos", None), P(), P(), P(), P("pos"), P("pos"))
    out_specs = (P(None, "gz", "pos", None), P(None, "pos", "gz", None))
    return jax.shard_map(body, mesh=mesh, in_specs=in_specs, out_specs=out_specs, check_vma=False)
```

profile of v0, /device:TPU:0, one launch (start us, length us, event | category | flops | bytes accessed | tf_op | source)
XLA Modules:
  0.0 248.1 jit_solution(8172619403252615749)
XLA Ops:
  0.6 0.0 copy-start
  0.6 1.5 fusion.45
  2.1 0.9 select_reduce_fusion
  3.0 0.2 slice_reduce_fusion.3
  3.2 3.7 %select_add_fusion = (f32[1,256,256]{2,1,0:T(8,128)S(1)}, pred[1,256,256]{2,1,0:T(8,128)(4,1)S(1)}, pred[1,256,256]{2,1,0:T(8,128)(4,1)S(1)}, pred[1,256,256]{2,1,0:T(8,128)(4,1)S(1)}, pred[1,256,256]{2,1,0:T(8,128)(4,1)S(1)}) fusion(f32[]{:T(128)} %bitcast.8, f32[]{:T(128)} %bitcast.7, f32[]{:T(128)} %bitcast.6, f32[]{:T(128)} %bitcast.5, ...), kind=kLoop, calls=%fused_computation.82 | loop fusion | flops 720896 | bytes 786448 | tf_op jit(solution)/shard_map/add | solution.py:95
  7.0 1.3 add_multiply_fusion
  8.3 2.4 collective-permute-start.1
  10.7 1.3 collective-permute-start.3
  12.0 5.1 %collective-permute-start = (f32[1,256,256]{2,1,0:T(8,128)S(1)}, f32[1,256,256]{2,1,0:T(8,128)S(1)}, u32[]{:S(2)}, u32[]{:S(2)}) collective-permute-start(f32[1,256,256]{2,1,0:T(8,128)S(1)} %get-tuple-element.24), channel_id=1, source_target_pairs={{0,1},{1,2},{2,3},{3,4},{4,5},{5,6},{6,7},{7,8},{8,9},{9,10},{10,1... | collective-permute-start | bytes 786440 | tf_op jit(solution)/shard_map/ppermute | solution.py:16
  17.2 1.3 collective-permute-start.2
  18.5 0.0 collective-permute-done
  18.5 3.3 %collective-permute-done.2 = f32[1,256,256]{2,1,0:T(8,128)S(1)} collective-permute-done((f32[1,256,256]{2,1,0:T(8,128)S(1)}, f32[1,256,256]{2,1,0:T(8,128)S(1)}, u32[]{:S(2)}, u32[]{:S(2)}) %collective-permute-start.2) | collective-permute-done | bytes 262176 | tf_op jit(solution)/shard_map/ppermute | solution.py:19
  21.8 0.4 select_maximum_fusion.4
  22.2 0.0 copy-start.2
  22.2 0.3 fusion.35
  22.5 0.0 copy-start.4
  22.5 0.0 copy-start.6
  22.6 0.0 copy-start.8
  22.6 0.0 copy-start.10
  22.6 0.0 copy-start.12
  22.6 0.0 copy-start.14
  22.6 0.0 collective-permute-done.1
  22.6 0.0 collective-permute-done.3
  22.6 2.4 select_maximum_fusion.2
  25.0 0.0 copy-done.2
  25.0 1.8 multiply_reduce_fusion.1
  26.8 0.0 copy-done.4
  26.8 0.0 copy-done.6
  26.8 0.0 copy-done.8
  26.9 0.0 copy-done.10
  26.9 0.0 copy-start.16
  26.9 50.9 %all-reduce.4 = (f32[4]{0:T(128)S(1)}, f32[4]{0:T(128)S(1)}) all-reduce(f32[4]{0:T(128)S(1)} %get-tuple-element.14, f32[4]{0:T(128)S(1)} %get-tuple-element.13), channel_id=1, replica_groups=mesh['pos'=2,'gz'=16] {'gz'}, use_global_device_ids=true, to_apply=%region_2.3 | all-reduce | flops 8 | bytes 64 | tf_op jit(solution)/shard_map/psum | solution.py:80
  77.8 0.6 multiply_reduce_fusion
  78.3 29.5 %psum.30 = f32[4]{0:T(128)S(1)} all-reduce(f32[4]{0:T(128)S(1)} %multiply_reduce_fusion), channel_id=1, replica_groups=mesh['pos'=2,'gz'=16] {'gz'}, use_global_device_ids=true, to_apply=%region_6.7 | all-reduce | flops 4 | bytes 32 | tf_op jit(solution)/shard_map/psum | solution.py:80
  107.8 0.5 multiply_add_fusion.1
  108.3 1.8 collective-permute-start.4
  110.2 1.3 collective-permute-start.5
  111.5 11.8 %gather_fusion = s32[2048]{0:T(1024)S(1)} fusion(s32[2048]{0:T(1024)S(1)} %copy-done, s32[2048]{0:T(1024)S(1)} %fusion.41), kind=kCustom, calls=%fused_computation.2 | custom fusion | bytes 24576 | tf_op jit(solution)/shard_map/jit(_take)/gather | solution.py:57
  123.3 0.0 copy-start.5
  123.3 0.0 copy-start.7
  123.4 0.0 collective-permute-done.4
  123.4 0.0 collective-permute-done.5
  123.4 3.5 %select_maximum_fusion = f32[4,3,258,258]{3,2,1,0:T(8,128)S(1)} fusion(f32[4,1,256,256]{3,2,1,0:T(8,128)} %collective-permute-done.5, f32[4,1,256,256]{3,2,1,0:T(8,128)S(1)} %multiply_add_fusion.1, f32[4,1,256,256]{3,2,1,0:T(8,128)S(1)} %collective-permute-done.4), kind=kLoop, calls=%fused_computation.7 | loop fusion | flops 11981520 | bytes 6340800 | tf_op jit(solution)/shard_map/concatenate | solution.py:20
  127.0 2.5 %fusion.13 = f32[4]{0:T(128)S(1)} fusion(f32[4,1,256,256]{3,2,1,0:T(8,128)S(1)} %multiply_add_fusion.1, f32[4,3,258,258]{3,2,1,0:T(8,128)S(1)} %select_maximum_fusion, f32[4,1,256,256]{3,2,1,0:T(8,128)} %collective-permute-done.5, f32[4,1,256,256]{3,2,1,0:T(8,128)S(1)} %collective-permute-done.4, f32[256,256]{1,0:T(8,128)S(1)} %copy-done.7, ...), kind=kLoop, calls=%fused_computation.35 | loop fusion | flops 5505020 | bytes 8912912 | tf_op jit(solution)/shard_map/reduce_sum | solution.py:72
  129.5 39.2 %psum.31 = f32[4]{0:T(128)S(1)} all-reduce(f32[4]{0:T(128)S(1)} %fusion.13), channel_id=1, replica_groups=mesh['pos'=2,'gz'=16] {'gz'}, use_global_device_ids=true, to_apply=%region_8.9 | all-reduce | flops 4 | bytes 32 | tf_op jit(solution)/shard_map/psum | solution.py:106
  168.8 0.4 multiply_add_fusion
  169.2 0.0 copy-start.3
  169.2 1.0 copy-done.3
  170.2 0.7 fusion.9
  170.9 16.5 %copy.33 = f32[4,1,256,256]{0,3,2,1:T(8,128)} copy(f32[4,1,256,256]{3,2,1,0:T(8,128)S(1)} %get-tuple-element.34) | data formatting | bytes 2097152 | tf_op jit(solution)/shard_map/mul | solution.py:55
  187.4 16.0 %gather_fusion.1 = f32[2048,4]{1,0:T(8,128)S(1)} fusion(f32[4,65536]{0,1:T(8,128)} %bitcast.64, s32[2048]{0:T(1024)S(1)} %fusion.42), kind=kCustom, calls=%fused_computation.clone | custom fusion | bytes 73728 | tf_op jit(solution)/shard_map/jit(_take)/gather | solution.py:58
  203.4 0.3 copy.34
  203.8 16.5 %copy.35 = f32[4,1,256,256]{0,3,2,1:T(8,128)} copy(f32[4,1,256,256]{3,2,1,0:T(8,128)S(1)} %get-tuple-element.33) | data formatting | bytes 2097152 | tf_op jit(solution)/shard_map/mul | solution.py:56
  220.3 16.0 %gather_fusion.2 = f32[2048,4]{1,0:T(8,128)S(1)} fusion(f32[4,65536]{0,1:T(8,128)} %bitcast.63, s32[2048]{0:T(1024)S(1)} %fusion.42), kind=kCustom, calls=%fused_computation.1.clone | custom fusion | bytes 73728 | tf_op jit(solution)/shard_map/jit(_take)/gather | solution.py:59
  236.3 0.3 copy.36
  236.6 0.1 subtract_bitcast_fusion.1
  236.7 0.1 reshape.211
  236.8 0.1 reduce_sum.61
  236.9 0.1 copy.37
  237.0 9.1 %all_to_all.4 = f32[8,1,32]{0,1,2:T(1,128)S(1)} all-to-all(f32[8,1,32]{0,1,2:T(1,128)S(1)} %copy.37), channel_id=1, replica_groups=mesh['pos'=2,'gz'=16] {'gz'}, dimensions={2} | all-to-all | bytes 2048 | tf_op jit(solution)/shard_map/all_to_all | solution.py:119
  246.1 0.5 broadcast.493
  246.6 0.7 reduce.12
  247.3 0.1 reshape.212
  247.4 0.7 copy.38
  (27 shorter events, 0.2 us)
Async XLA Ops:
  0.6 110.9 %copy-start = (s32[2048]{0:T(1024)S(1)}, s32[2048]{0:T(1024)}, u32[]{:S(2)}) copy-start(s32[2048]{0:T(1024)} %param.14) | copy-start | bytes 24580
  8.3 14.3 %collective-permute-start.1 = (f32[4,1,256,256]{3,2,1,0:T(8,128)S(1)}, f32[4,1,256,256]{3,2,1,0:T(8,128)S(1)}, u32[]{:S(2)}, u32[]{:S(2)}) collective-permute-start(f32[4,1,256,256]{3,2,1,0:T(8,128)S(1)} %add_multiply_fusion), channel_id=1, source_target_pairs={{0,1},{1,2},{2,3},{3,4},{4,5},{5,6},{6,7},{7,8},{8,9},{9,10},{10,1... | collective-permute-start | bytes 3145736 | tf_op jit(solution)/shard_map/ppermute | solution.py:16
  10.7 11.9 %collective-permute-start.3 = (f32[4,1,256,256]{3,2,1,0:T(8,128)S(1)}, f32[4,1,256,256]{3,2,1,0:T(8,128)S(1)}, u32[]{:S(2)}, u32[]{:S(2)}) collective-permute-start(f32[4,1,256,256]{3,2,1,0:T(8,128)S(1)} %add_multiply_fusion), channel_id=1, source_target_pairs={{1,0},{2,1},{3,2},{4,3},{5,4},{6,5},{7,6},{8,7},{9,8},{10,9},{11,1... | collective-permute-start | bytes 3145736 | tf_op jit(solution)/shard_map/ppermute | solution.py:19
  12.0 6.4 %collective-permute-start = (f32[1,256,256]{2,1,0:T(8,128)S(1)}, f32[1,256,256]{2,1,0:T(8,128)S(1)}, u32[]{:S(2)}, u32[]{:S(2)}) collective-permute-start(f32[1,256,256]{2,1,0:T(8,128)S(1)} %get-tuple-element.24), channel_id=1, source_target_pairs={{0,1},{1,2},{2,3},{3,4},{4,5},{5,6},{6,7},{7,8},{8,9},{9,10},{10,1... | collective-permute-start | bytes 786440 | tf_op jit(solution)/shard_map/ppermute | solution.py:16
  17.2 4.7 %collective-permute-start.2 = (f32[1,256,256]{2,1,0:T(8,128)S(1)}, f32[1,256,256]{2,1,0:T(8,128)S(1)}, u32[]{:S(2)}, u32[]{:S(2)}) collective-permute-start(f32[1,256,256]{2,1,0:T(8,128)S(1)} %get-tuple-element.24), channel_id=1, source_target_pairs={{1,0},{2,1},{3,2},{4,3},{5,4},{6,5},{7,6},{8,7},{9,8},{10,9},{11,1... | collective-permute-start | bytes 786440 | tf_op jit(solution)/shard_map/ppermute | solution.py:19
  22.2 2.8 %copy-start.2 = (f32[1,256,256]{2,1,0:T(8,128)S(1)}, f32[1,256,256]{2,1,0:T(8,128)}, u32[]{:S(2)}) copy-start(f32[1,256,256]{2,1,0:T(8,128)} %param.9) | copy-start | bytes 786436
  22.5 4.3 %copy-start.4 = (f32[256,256]{1,0:T(8,128)}, f32[256,256]{1,0:T(8,128)S(1)}, u32[]{:S(2)}) copy-start(f32[256,256]{1,0:T(8,128)S(1)} %get-tuple-element.29) | copy-start | bytes 786436
  22.5 4.3 %copy-start.6 = (f32[256,256]{1,0:T(8,128)}, f32[256,256]{1,0:T(8,128)S(1)}, u32[]{:S(2)}) copy-start(f32[256,256]{1,0:T(8,128)S(1)} %get-tuple-element.30) | copy-start | bytes 786436
  22.6 4.3 %copy-start.8 = (f32[256,256]{1,0:T(8,128)}, f32[256,256]{1,0:T(8,128)S(1)}, u32[]{:S(2)}) copy-start(f32[256,256]{1,0:T(8,128)S(1)} %get-tuple-element.31) | copy-start | bytes 786436
  22.6 4.3 %copy-start.10 = (f32[256,256]{1,0:T(8,128)}, f32[256,256]{1,0:T(8,128)S(1)}, u32[]{:S(2)}) copy-start(f32[256,256]{1,0:T(8,128)S(1)} %get-tuple-element.32) | copy-start | bytes 786436
  22.6 4.3 %copy-start.12 = (f32[256,256]{1,0:T(8,128)}, f32[256,256]{1,0:T(8,128)S(1)}, u32[]{:S(2)}) copy-start(f32[256,256]{1,0:T(8,128)S(1)} %get-tuple-element.35) | copy-start | bytes 786436
  22.6 4.3 %copy-start.14 = (f32[256,256]{1,0:T(8,128)}, f32[256,256]{1,0:T(8,128)S(1)}, u32[]{:S(2)}) copy-start(f32[256,256]{1,0:T(8,128)S(1)} %get-tuple-element.36) | copy-start | bytes 786436
  26.9 84.6 %copy-start.16 = (s32[2048]{0:T(1024)S(1)}, s32[2048]{0:T(1024)}, u32[]{:S(2)}) copy-start(s32[2048]{0:T(1024)} %param.15) | copy-start | bytes 24580
  108.3 15.1 %collective-permute-start.4 = (f32[4,1,256,256]{3,2,1,0:T(8,128)S(1)}, f32[4,1,256,256]{3,2,1,0:T(8,128)S(1)}, u32[]{:S(2)}, u32[]{:S(2)}) collective-permute-start(f32[4,1,256,256]{3,2,1,0:T(8,128)S(1)} %multiply_add_fusion.1), channel_id=1, source_target_pairs={{0,1},{1,2},{2,3},{3,4},{4,5},{5,6},{6,7},{7,8},{8,9},{9,10},{10,1... | collective-permute-start | bytes 3145736 | tf_op jit(solution)/shard_map/ppermute | solution.py:16
  110.2 13.3 %collective-permute-start.5 = (f32[4,1,256,256]{3,2,1,0:T(8,128)S(1)}, f32[4,1,256,256]{3,2,1,0:T(8,128)}, u32[]{:S(2)}, u32[]{:S(2)}) collective-permute-start(f32[4,1,256,256]{3,2,1,0:T(8,128)S(1)} %multiply_add_fusion.1), channel_id=1, source_target_pairs={{1,0},{2,1},{3,2},{4,3},{5,4},{6,5},{7,6},{8,7},{9,8},{10,9},{11,1... | collective-permute-start | bytes 3145736 | tf_op jit(solution)/shard_map/ppermute | solution.py:19
  123.3 3.7 %copy-start.5 = (f32[256,256]{1,0:T(8,128)S(1)}, f32[256,256]{1,0:T(8,128)}, u32[]{:S(2)}) copy-start(f32[256,256]{1,0:T(8,128)} %copy-done.4) | copy-start | bytes 786436
  123.3 3.7 %copy-start.7 = (f32[256,256]{1,0:T(8,128)S(1)}, f32[256,256]{1,0:T(8,128)}, u32[]{:S(2)}) copy-start(f32[256,256]{1,0:T(8,128)} %copy-done.6) | copy-start | bytes 786436
  123.3 3.7 %copy-start.9 = (f32[256,256]{1,0:T(8,128)S(1)}, f32[256,256]{1,0:T(8,128)}, u32[]{:S(2)}) copy-start(f32[256,256]{1,0:T(8,128)} %copy-done.8) | copy-start | bytes 786436
  123.3 3.7 %copy-start.11 = (f32[256,256]{1,0:T(8,128)S(1)}, f32[256,256]{1,0:T(8,128)}, u32[]{:S(2)}) copy-start(f32[256,256]{1,0:T(8,128)} %copy-done.10) | copy-start | bytes 786436
  123.3 3.7 %copy-start.13 = (f32[256,256]{1,0:T(8,128)S(1)}, f32[256,256]{1,0:T(8,128)}, u32[]{:S(2)}) copy-start(f32[256,256]{1,0:T(8,128)} %copy-done.12) | copy-start | bytes 786436
  123.3 3.7 %copy-start.15 = (f32[256,256]{1,0:T(8,128)S(1)}, f32[256,256]{1,0:T(8,128)}, u32[]{:S(2)}) copy-start(f32[256,256]{1,0:T(8,128)} %copy-done.14) | copy-start | bytes 786436
  169.2 1.0 copy-start.3
  203.8 44.3 %copy-start.1 = (s32[2048]{0:T(1024)S(1)}, s32[2048]{0:T(1024)}, u32[]{:S(2)}) copy-start(s32[2048]{0:T(1024)} %param.14) | copy-start | bytes 24580
where the time goes:
time: 249 us; the launch traced here: 248 us
  blocking collectives  129 us (52%)
  local copies, waits for them, and re-layouts  81.7 us (33%)
  other arithmetic  20.1 us (8%)
  starting transfers between devices  13.2 us (5%)
  waiting for transfers between devices  3.36 us (1%)
    psum x2, blocking collectives, squares(): return lax.psum(column_sum(residual, residual), 'gz')  80.3 us
    psum x1, blocking collectives, body(): curvature = lax.psum(column_sum(direction, image), 'gz')  39.2 us
    mul x1, local copies, waits for them, and re-layouts, band_stress(): flux_x = 0.5 * (padded[:, :, 1:-1, 2:] - padded[:, :, 1:-1, :-2])  16.5 us
    mul x1, local copies, waits for them, and re-layouts, band_stress(): flux_y = -0.5 * (padded[:, :, 2:, 1:-1] - padded[:, :, :-2, 1:-1])  16.5 us
    gather x2, local copies, waits for them, and re-layouts, band_stress(): jnp.take(flux_x.reshape(count_cols, depth, width_x * width_y), ordered, a...  16.3 us
    gather x2, local copies, waits for them, and re-layouts, band_stress(): jnp.take(flux_y.reshape(count_cols, depth, width_x * width_y), ordered, a...  16.3 us
    gather x1, local copies, waits for them, and re-layouts, band_stress(): ordered = jnp.take(band_cells, sector_order)  11.8 us
    ppermute x3, starting transfers between devices, with_halo(): lax.ppermute(lax.slice_in_dim(block, block.shape[dim] - width, None, axis...  9.37 us
  transfers between devices with their start and end apart: 6, of which 1 were waited for; matrix products, arithmetic and copies ran while one was open for 5% of the time, Pallas kernels for 0%

commit v1 on v0

--- a/solution.py
+++ b/solution.py
@@ -6,6 +6,29 @@
 ITERS = 2
 PER_SEC = 64
 MASS_SHIFT = 0.5
+
+
+def split_up(shard, dim, count):
+    shape = shard.shape
+    tiles = shard.reshape(*shape[:dim], count, shape[dim] // count, *shape[dim + 1 :])
+    return jnp.moveaxis(tiles, dim, 0)
+
+
+def laid_out(parts, dim):
+    dims = list(parts.shape[1:])
+    dims[dim] *= parts.shape[0]
+    return jnp.moveaxis(parts, 0, dim).reshape(dims)
+
+
+def pairwise_exchange(array, axis, split_dim, concat_dim):
+    size, mine = (lax.axis_size(axis), lax.axis_index(axis))
+    blocks = split_up(array, split_dim, size)
+    outs = [blocks[mine]]
+    for step in range(1, size):
+        sent = blocks[mine ^ step]
+        outs.append(lax.ppermute(sent, axis, [(i, i ^ step) for i in range(size)]))
+    blocks = jnp.stack(outs)[mine ^ jnp.arange(size)]
+    return laid_out(blocks, concat_dim)
 
 
 def with_halo(block, sides, width):
@@ -116,7 +139,7 @@
     band_total = stress.shape[3]
     cell_forces = stress.reshape(2 * count_cols, depth, band_total // PER_SEC, PER_SEC)
     sector_sums = jnp.sum(cell_forces, axis=-1)
-    gathered = lax.all_to_all(sector_sums, "gz", split_axis=2, concat_axis=1, tiled=True)
+    gathered = pairwise_exchange(sector_sums, "gz", 2, 1)
     full_depth = gathered.shape[1]
     local_sectors = gathered.shape[2]
     return (

time: 249 us -> 267 us (1.072)
  starting transfers between devices: 13.2 us -> 34.4 us
  blocking collectives: 129 us -> 120 us
  other arithmetic: 20.1 us -> 25.8 us
    ppermute x0 -> x15, starting transfers between devices: none -> 20.5 us  [pairwise_exchange(): outs.append(lax.ppermute(sent, axis, [(i, i ^ step) for i in range(size)]))]
    all_to_all x1 -> x0, blocking collectives: 9.06 us -> none  [body(): lax.all_to_all(sector_sums, 'gz', split_axis=2, concat_axis=1, tiled=True)]
  transfers between devices with their start and end apart: 6 -> 21, of which waited for: 1 -> 2; matrix products, arithmetic and copies ran while one was open for 5% -> 6% of each run, Pallas kernels for 0% -> 0%
where the time goes in v1:
time: 267 us; the launch traced here: 266 us
  blocking collectives  120 us (45%)
  local copies, waits for them, and re-layouts  81.1 us (30%)
  starting transfers between devices  34.4 us (13%)
  other arithmetic  25.8 us (10%)
  waiting for transfers between devices  3.84 us (1%)
    psum x2, blocking collectives, squares(): return lax.psum(column_sum(residual, residual), 'gz')  80.5 us
    psum x1, blocking collectives, body(): curvature = lax.psum(column_sum(direction, image), 'gz')  39 us
    ppermute x15, starting transfers between devices, pairwise_exchange(): outs.append(lax.ppermute(sent, axis, [(i, i ^ step) for i in range(size)]))  20.5 us
    mul x1, local copies, waits for them, and re-layouts, band_stress(): flux_x = 0.5 * (padded[:, :, 1:-1, 2:] - padded[:, :, 1:-1, :-2])  16.6 us
    mul x1, local copies, waits for them, and re-layouts, band_stress(): flux_y = -0.5 * (padded[:, :, 2:, 1:-1] - padded[:, :, :-2, 1:-1])  16.6 us
    gather x2, local copies, waits for them, and re-layouts, band_stress(): jnp.take(flux_x.reshape(count_cols, depth, width_x * width_y), ordered, a...  16.3 us
    gather x2, local copies, waits for them, and re-layouts, band_stress(): jnp.take(flux_y.reshape(count_cols, depth, width_x * width_y), ordered, a...  16.3 us
    gather x1, local copies, waits for them, and re-layouts, band_stress(): ordered = jnp.take(band_cells, sector_order)  11.8 us
  transfers between devices with their start and end apart: 21, of which 2 were waited for; matrix products, arithmetic and copies ran while one was open for 6% of the time, Pallas kernels for 0%

profile of v1, /device:TPU:0, one launch (start us, length us, event | category | flops | bytes accessed | tf_op | source)
XLA Modules:
  0.0 266.0 jit_solution(5032191866792451002)
XLA Ops:
  0.6 0.0 copy-start
  0.6 1.5 fusion.62
  2.1 0.9 select_reduce_fusion
  3.0 0.2 slice_reduce_fusion.3
  3.2 3.7 %select_add_fusion = (f32[1,256,256]{2,1,0:T(8,128)S(1)}, pred[1,256,256]{2,1,0:T(8,128)(4,1)S(1)}, pred[1,256,256]{2,1,0:T(8,128)(4,1)S(1)}, pred[1,256,256]{2,1,0:T(8,128)(4,1)S(1)}, pred[1,256,256]{2,1,0:T(8,128)(4,1)S(1)}) fusion(f32[]{:T(128)} %bitcast.8, f32[]{:T(128)} %bitcast.7, f32[]{:T(128)} %bitcast.6, f32[]{:T(128)} %bitcast.5, ...), kind=kLoop, calls=%fused_computation.83 | loop fusion | flops 720896 | bytes 786448 | tf_op jit(solution)/shard_map/add | solution.py:118
  7.0 2.3 add_multiply_fusion
  9.3 2.4 collective-permute-start.1
  11.7 1.3 collective-permute-start.3
  13.0 5.8 %collective-permute-start = (f32[1,256,256]{2,1,0:T(8,128)S(1)}, f32[1,256,256]{2,1,0:T(8,128)}, u32[]{:S(2)}, u32[]{:S(2)}) collective-permute-start(f32[1,256,256]{2,1,0:T(8,128)S(1)} %get-tuple-element.26), channel_id=1, source_target_pairs={{0,1},{1,2},{2,3},{3,4},{4,5},{5,6},{6,7},{7,8},{8,9},{9,10},{10,1... | collective-permute-start | bytes 786440 | tf_op jit(solution)/shard_map/ppermute | solution.py:39
  18.8 1.3 collective-permute-start.2
  20.1 0.7 fusion.41
  20.8 0.0 collective-permute-done
  20.8 2.1 collective-permute-done.2
  22.9 1.4 select_maximum_fusion.4
  24.3 0.0 copy-start.2
  24.3 1.4 fusion.35
  25.9 0.0 collective-permute-done.1
  25.9 0.0 collective-permute-done.3
  25.9 3.8 %select_maximum_fusion.2 = f32[4,3,258,258]{3,2,1,0:T(8,128)S(1)} fusion(f32[4,1,256,256]{3,2,1,0:T(8,128)S(1)} %collective-permute-done.3, f32[4,1,256,256]{3,2,1,0:T(8,128)} %add_multiply_fusion, f32[4,1,256,256]{3,2,1,0:T(8,128)S(1)} %collective-permute-done.1), kind=kLoop, calls=%fused_computation.10 | loop fusion | flops 11981520 | bytes 6340800 | tf_op jit(solution)/shard_map/concatenate | solution.py:43
  29.7 3.0 %multiply_reduce_fusion.1 = (f32[4]{0:T(128)S(1)}, f32[4]{0:T(128)S(1)}, f32[4,1,256,256]{3,2,1,0:T(8,128)S(1)}) fusion(f32[4,3,258,258]{3,2,1,0:T(8,128)S(1)} %select_maximum_fusion.2, f32[256,256]{1,0:T(8,128)S(1)} %get-tuple-element.32, f32[256,256]{1,0:T(8,128)S(1)} %get-tuple-element.33, f32[256,256]{1,0:T(8,128)S(1)} %get-tuple-element.34, ...), kind=kLoop, calls=%fused_computation.62 | loop fusion | flops 8126456 | bytes 10223712 | tf_op jit(solution)/shard_map/reduce_sum | solution.py:95
  32.7 51.0 %all-reduce.4 = (f32[4]{0:T(128)S(1)}, f32[4]{0:T(128)S(1)}) all-reduce(f32[4]{0:T(128)S(1)} %get-tuple-element.16, f32[4]{0:T(128)S(1)} %get-tuple-element.15), channel_id=1, replica_groups=mesh['pos'=2,'gz'=16] {'gz'}, use_global_device_ids=true, to_apply=%region_2.3 | all-reduce | flops 8 | bytes 64 | tf_op jit(solution)/shard_map/psum | solution.py:103
  83.8 0.6 multiply_reduce_fusion
  84.4 29.5 %psum.30 = f32[4]{0:T(128)S(1)} all-reduce(f32[4]{0:T(128)S(1)} %multiply_reduce_fusion), channel_id=1, replica_groups=mesh['pos'=2,'gz'=16] {'gz'}, use_global_device_ids=true, to_apply=%region_6.7 | all-reduce | flops 4 | bytes 32 | tf_op jit(solution)/shard_map/psum | solution.py:103
  113.8 0.5 multiply_add_fusion.1
  114.3 0.0 copy-start.18
  114.3 1.8 collective-permute-start.4
  116.2 1.3 collective-permute-start.5
  117.6 11.8 %gather_fusion = s32[2048]{0:T(1024)S(1)} fusion(s32[2048]{0:T(1024)S(1)} %copy-done, s32[2048]{0:T(1024)S(1)} %fusion.41), kind=kCustom, calls=%fused_computation.2 | custom fusion | bytes 24576 | tf_op jit(solution)/shard_map/jit(_take)/gather | solution.py:80
  129.6 0.0 collective-permute-done.5
  129.6 3.5 %select_maximum_fusion = f32[4,3,258,258]{3,2,1,0:T(8,128)S(1)} fusion(f32[4,1,256,256]{3,2,1,0:T(8,128)} %collective-permute-done.5, f32[4,1,256,256]{3,2,1,0:T(8,128)S(1)} %multiply_add_fusion.1, f32[4,1,256,256]{3,2,1,0:T(8,128)S(1)} %collective-permute-done.4), kind=kLoop, calls=%fused_computation.8 | loop fusion | flops 11981520 | bytes 6340800 | tf_op jit(solution)/shard_map/concatenate | solution.py:43
  133.2 2.5 fusion.13
  135.7 39.0 %psum.31 = f32[4]{0:T(128)S(1)} all-reduce(f32[4]{0:T(128)S(1)} %fusion.13), channel_id=1, replica_groups=mesh['pos'=2,'gz'=16] {'gz'}, use_global_device_ids=true, to_apply=%region_8.9 | all-reduce | flops 4 | bytes 32 | tf_op jit(solution)/shard_map/psum | solution.py:129
  174.8 0.4 multiply_add_fusion
  175.2 0.0 copy-start.4
  175.2 0.7 fusion.9
  176.0 16.6 %copy.60 = f32[4,1,256,256]{0,3,2,1:T(8,128)} copy(f32[4,1,256,256]{3,2,1,0:T(8,128)S(1)} %get-tuple-element.36) | data formatting | bytes 2097152 | tf_op jit(solution)/shard_map/mul | solution.py:78
  192.6 16.0 %gather_fusion.2 = f32[2048,4]{1,0:T(8,128)S(1)} fusion(f32[4,65536]{0,1:T(8,128)} %bitcast.134, s32[2048]{0:T(1024)S(1)} %fusion.42), kind=kCustom, calls=%fused_computation.clone | custom fusion | bytes 73728 | tf_op jit(solution)/shard_map/jit(_take)/gather | solution.py:81
  208.6 0.3 copy.61
  208.9 16.6 %copy.62 = f32[4,1,256,256]{0,3,2,1:T(8,128)} copy(f32[4,1,256,256]{3,2,1,0:T(8,128)S(1)} %get-tuple-element.35) | data formatting | bytes 2097152 | tf_op jit(solution)/shard_map/mul | solution.py:79
  225.5 16.0 %gather_fusion.3 = f32[2048,4]{1,0:T(8,128)S(1)} fusion(f32[4,65536]{0,1:T(8,128)} %bitcast.133, s32[2048]{0:T(1024)S(1)} %fusion.42), kind=kCustom, calls=%fused_computation.1.clone | custom fusion | bytes 73728 | tf_op jit(solution)/shard_map/jit(_take)/gather | solution.py:82
  241.6 0.3 copy.63
  241.9 0.1 subtract_bitcast_fusion.1
  242.0 0.1 reshape.255
  242.1 0.1 reduce_sum.59
  242.2 0.1 copy.64
  242.3 0.1 collective-permute-start.6
  242.4 0.1 collective-permute-start.7
  242.5 1.8 collective-permute-start.8
  244.3 0.0 collective-permute-start.9
  244.3 1.7 collective-permute-start.10
  246.0 0.0 collective-permute-done.6
  246.0 0.1 collective-permute-start.11
  246.0 0.0 collective-permute-done.7
  246.0 2.6 collective-permute-start.12
  248.7 2.6 collective-permute-start.14
  251.3 0.1 collective-permute-start.15
  251.4 3.5 %collective-permute-start.16 = (f32[8,1,2]{0,2,1:T(2,128)S(1)}, f32[8,1,2]{0,2,1:T(2,128)S(1)}, u32[]{:S(2)}, u32[]{:S(2)}) collective-permute-start(f32[8,1,2]{0,2,1:T(2,128)S(1)} %get-tuple-element.45), channel_id=1, source_target_pairs={{0,11},{1,10},{2,9},{3,8},{4,15},{5,14},{6,13},{7,12},{8,3},{9,2},... | collective-permute-start | bytes 200 | tf_op jit(solution)/shard_map/ppermute | solution.py:29
  255.0 3.5 %collective-permute-start.18 = (f32[8,1,2]{0,2,1:T(2,128)S(1)}, f32[8,1,2]{0,2,1:T(2,128)S(1)}, u32[]{:S(2)}, u32[]{:S(2)}) collective-permute-start(f32[8,1,2]{0,2,1:T(2,128)S(1)} %get-tuple-element.43), channel_id=1, source_target_pairs={{0,13},{1,12},{2,15},{3,14},{4,9},{5,8},{6,11},{7,10},{8,5},{9,4},... | collective-permute-start | bytes 200 | tf_op jit(solution)/shard_map/ppermute | solution.py:29
  258.4 0.2 collective-permute-start.19
  258.7 4.3 %collective-permute-start.20 = (f32[8,1,2]{0,2,1:T(2,128)S(1)}, f32[8,1,2]{0,2,1:T(2,128)S(1)}, u32[]{:S(2)}, u32[]{:S(2)}) collective-permute-start(f32[8,1,2]{0,2,1:T(2,128)S(1)} %get-tuple-element.41), channel_id=1, source_target_pairs={{0,15},{1,14},{2,13},{3,12},{4,11},{5,10},{6,9},{7,8},{8,7},{9,6},... | collective-permute-start | bytes 200 | tf_op jit(solution)/shard_map/ppermute | solution.py:29
  263.0 1.7 collective-permute-done.19
  264.7 0.6 gather_fusion.1
  265.3 0.1 copy.65
  265.4 0.6 copy.66
  (78 shorter events, 0.4 us)
Async XLA Ops:
  0.6 116.9 %copy-start = (s32[2048]{0:T(1024)S(1)}, s32[2048]{0:T(1024)}, u32[]{:S(2)}) copy-start(s32[2048]{0:T(1024)} %param.14) | copy-start | bytes 24580
  6.9 16.0 %copy-start.17 = (f32[1,256,256]{2,1,0:T(8,128)}, f32[1,256,256]{2,1,0:T(8,128)S(1)}, u32[]{:S(2)}) copy-start(f32[1,256,256]{2,1,0:T(8,128)S(1)} %get-tuple-element.26) | copy-start | bytes 786436
  9.3 16.6 %collective-permute-start.1 = (f32[4,1,256,256]{3,2,1,0:T(8,128)}, f32[4,1,256,256]{3,2,1,0:T(8,128)S(1)}, u32[]{:S(2)}, u32[]{:S(2)}) collective-permute-start(f32[4,1,256,256]{3,2,1,0:T(8,128)} %add_multiply_fusion), channel_id=1, source_target_pairs={{0,1},{1,2},{2,3},{3,4},{4,5},{5,6},{6,7},{7,8},{8,9},{9,10},{10,1... | collective-permute-start | bytes 3145736 | tf_op jit(solution)/shard_map/ppermute | solution.py:39
  11.7 14.2 %collective-permute-start.3 = (f32[4,1,256,256]{3,2,1,0:T(8,128)}, f32[4,1,256,256]{3,2,1,0:T(8,128)S(1)}, u32[]{:S(2)}, u32[]{:S(2)}) collective-permute-start(f32[4,1,256,256]{3,2,1,0:T(8,128)} %add_multiply_fusion), channel_id=1, source_target_pairs={{1,0},{2,1},{3,2},{4,3},{5,4},{6,5},{7,6},{8,7},{9,8},{10,9},{11,1... | collective-permute-start | bytes 3145736 | tf_op jit(solution)/shard_map/ppermute | solution.py:42
  13.0 7.8 %collective-permute-start = (f32[1,256,256]{2,1,0:T(8,128)S(1)}, f32[1,256,256]{2,1,0:T(8,128)}, u32[]{:S(2)}, u32[]{:S(2)}) collective-permute-start(f32[1,256,256]{2,1,0:T(8,128)S(1)} %get-tuple-element.26), channel_id=1, source_target_pairs={{0,1},{1,2},{2,3},{3,4},{4,5},{5,6},{6,7},{7,8},{8,9},{9,10},{10,1... | collective-permute-start | bytes 786440 | tf_op jit(solution)/shard_map/ppermute | solution.py:39
  18.8 4.1 %collective-permute-start.2 = (f32[1,256,256]{2,1,0:T(8,128)S(1)}, f32[1,256,256]{2,1,0:T(8,128)}, u32[]{:S(2)}, u32[]{:S(2)}) collective-permute-start(f32[1,256,256]{2,1,0:T(8,128)S(1)} %get-tuple-element.26), channel_id=1, source_target_pairs={{1,0},{2,1},{3,2},{4,3},{5,4},{6,5},{7,6},{8,7},{9,8},{10,9},{11,1... | collective-permute-start | bytes 786440 | tf_op jit(solution)/shard_map/ppermute | solution.py:42
  24.3 5.3 %copy-start.2 = (f32[1,256,256]{2,1,0:T(8,128)S(1)}, f32[1,256,256]{2,1,0:T(8,128)}, u32[]{:S(2)}) copy-start(f32[1,256,256]{2,1,0:T(8,128)} %param.9) | copy-start | bytes 786436
  25.8 6.9 %copy-start.5 = (f32[256,256]{1,0:T(8,128)}, f32[256,256]{1,0:T(8,128)S(1)}, u32[]{:S(2)}) copy-start(f32[256,256]{1,0:T(8,128)S(1)} %get-tuple-element.31) | copy-start | bytes 786436
  25.8 6.9 %copy-start.7 = (f32[256,256]{1,0:T(8,128)}, f32[256,256]{1,0:T(8,128)S(1)}, u32[]{:S(2)}) copy-start(f32[256,256]{1,0:T(8,128)S(1)} %get-tuple-element.32) | copy-start | bytes 786436
  25.8 6.9 %copy-start.9 = (f32[256,256]{1,0:T(8,128)}, f32[256,256]{1,0:T(8,128)S(1)}, u32[]{:S(2)}) copy-start(f32[256,256]{1,0:T(8,128)S(1)} %get-tuple-element.33) | copy-start | bytes 786436
  25.8 6.9 %copy-start.11 = (f32[256,256]{1,0:T(8,128)}, f32[256,256]{1,0:T(8,128)S(1)}, u32[]{:S(2)}) copy-start(f32[256,256]{1,0:T(8,128)S(1)} %get-tuple-element.34) | copy-start | bytes 786436
  25.8 6.9 %copy-start.13 = (f32[256,256]{1,0:T(8,128)}, f32[256,256]{1,0:T(8,128)S(1)}, u32[]{:S(2)}) copy-start(f32[256,256]{1,0:T(8,128)S(1)} %get-tuple-element.37) | copy-start | bytes 786436
  25.8 6.9 %copy-start.15 = (f32[256,256]{1,0:T(8,128)}, f32[256,256]{1,0:T(8,128)S(1)}, u32[]{:S(2)}) copy-start(f32[256,256]{1,0:T(8,128)S(1)} %get-tuple-element.38) | copy-start | bytes 786436
  25.9 3.8 %copy-start.3 = (f32[4,1,256,256]{3,2,1,0:T(8,128)}, f32[4,1,256,256]{3,2,1,0:T(8,128)S(1)}, u32[]{:S(2)}) copy-start(f32[4,1,256,256]{3,2,1,0:T(8,128)S(1)} %collective-permute-done.3) | copy-start | bytes 3145732
  114.3 15.2 %copy-start.18 = (s32[2048]{0:T(1024)S(1)}, s32[2048]{0:T(1024)}, u32[]{:S(2)}) copy-start(s32[2048]{0:T(1024)} %param.15) | copy-start | bytes 24580
  114.3 15.3 %collective-permute-start.4 = (f32[4,1,256,256]{3,2,1,0:T(8,128)S(1)}, f32[4,1,256,256]{3,2,1,0:T(8,128)S(1)}, u32[]{:S(2)}, u32[]{:S(2)}) collective-permute-start(f32[4,1,256,256]{3,2,1,0:T(8,128)S(1)} %multiply_add_fusion.1), channel_id=1, source_target_pairs={{0,1},{1,2},{2,3},{3,4},{4,5},{5,6},{6,7},{7,8},{8,9},{9,10},{10,1... | collective-permute-start | bytes 3145736 | tf_op jit(solution)/shard_map/ppermute | solution.py:39
  116.2 13.4 %collective-permute-start.5 = (f32[4,1,256,256]{3,2,1,0:T(8,128)S(1)}, f32[4,1,256,256]{3,2,1,0:T(8,128)}, u32[]{:S(2)}, u32[]{:S(2)}) collective-permute-start(f32[4,1,256,256]{3,2,1,0:T(8,128)S(1)} %multiply_add_fusion.1), channel_id=1, source_target_pairs={{1,0},{2,1},{3,2},{4,3},{5,4},{6,5},{7,6},{8,7},{9,8},{10,9},{11,1... | collective-permute-start | bytes 3145736 | tf_op jit(solution)/shard_map/ppermute | solution.py:42
  129.4 3.7 %copy-start.6 = (f32[256,256]{1,0:T(8,128)S(1)}, f32[256,256]{1,0:T(8,128)}, u32[]{:S(2)}) copy-start(f32[256,256]{1,0:T(8,128)} %copy-done.5) | copy-start | bytes 786436
  129.5 3.7 %copy-start.8 = (f32[256,256]{1,0:T(8,128)S(1)}, f32[256,256]{1,0:T(8,128)}, u32[]{:S(2)}) copy-start(f32[256,256]{1,0:T(8,128)} %copy-done.7) | copy-start | bytes 786436
  129.5 3.7 %copy-start.10 = (f32[256,256]{1,0:T(8,128)S(1)}, f32[256,256]{1,0:T(8,128)}, u32[]{:S(2)}) copy-start(f32[256,256]{1,0:T(8,128)} %copy-done.9) | copy-start | bytes 786436
  129.5 3.7 %copy-start.12 = (f32[256,256]{1,0:T(8,128)S(1)}, f32[256,256]{1,0:T(8,128)}, u32[]{:S(2)}) copy-start(f32[256,256]{1,0:T(8,128)} %copy-done.11) | copy-start | bytes 786436
  129.5 3.7 %copy-start.14 = (f32[256,256]{1,0:T(8,128)S(1)}, f32[256,256]{1,0:T(8,128)}, u32[]{:S(2)}) copy-start(f32[256,256]{1,0:T(8,128)} %copy-done.13) | copy-start | bytes 786436
  129.5 3.7 %copy-start.16 = (f32[256,256]{1,0:T(8,128)S(1)}, f32[256,256]{1,0:T(8,128)}, u32[]{:S(2)}) copy-start(f32[256,256]{1,0:T(8,128)} %copy-done.15) | copy-start | bytes 786436
  175.2 17.4 %copy-start.4 = (f32[4,1,256,256]{3,2,1,0:T(8,128)}, f32[4,1,256,256]{3,2,1,0:T(8,128)S(1)}, u32[]{:S(2)}) copy-start(f32[4,1,256,256]{3,2,1,0:T(8,128)S(1)} %multiply_add_fusion) | copy-start | bytes 3145732
  208.9 57.1 %copy-start.1 = (s32[2048]{0:T(1024)S(1)}, s32[2048]{0:T(1024)}, u32[]{:S(2)}) copy-start(s32[2048]{0:T(1024)} %param.14) | copy-start | bytes 24580
  242.3 3.7 %collective-permute-start.6 = (f32[8,1,2]{0,2,1:T(2,128)S(1)}, f32[8,1,2]{0,2,1:T(2,128)S(1)}, u32[]{:S(2)}, u32[]{:S(2)}) collective-permute-start(f32[8,1,2]{0,2,1:T(2,128)S(1)} %get-tuple-element.55), channel_id=1, source_target_pairs={{0,1},{1,0},{2,3},{3,2},{4,5},{5,4},{6,7},{7,6},{8,9},{9,8},{10,11... | collective-permute-start | bytes 200 | tf_op jit(solution)/shard_map/ppermute | solution.py:29
  242.4 3.6 %collective-permute-start.7 = (f32[8,1,2]{0,2,1:T(2,128)S(1)}, f32[8,1,2]{0,2,1:T(2,128)S(1)}, u32[]{:S(2)}, u32[]{:S(2)}) collective-permute-start(f32[8,1,2]{0,2,1:T(2,128)S(1)} %get-tuple-element.54), channel_id=1, source_target_pairs={{0,2},{1,3},{2,0},{3,1},{4,6},{5,7},{6,4},{7,5},{8,10},{9,11},{10,... | collective-permute-start | bytes 200 | tf_op jit(solution)/shard_map/ppermute | solution.py:29
  242.5 6.2 %collective-permute-start.8 = (f32[8,1,2]{0,2,1:T(2,128)S(1)}, f32[8,1,2]{0,2,1:T(2,128)S(1)}, u32[]{:S(2)}, u32[]{:S(2)}) collective-permute-start(f32[8,1,2]{0,2,1:T(2,128)S(1)} %get-tuple-element.53), channel_id=1, source_target_pairs={{0,3},{1,2},{2,1},{3,0},{4,7},{5,6},{6,5},{7,4},{8,11},{9,10},{10,... | collective-permute-start | bytes 200 | tf_op jit(solution)/shard_map/ppermute | solution.py:29
  244.3 4.5 %collective-permute-start.9 = (f32[8,1,2]{0,2,1:T(2,128)S(1)}, f32[8,1,2]{0,2,1:T(2,128)S(1)}, u32[]{:S(2)}, u32[]{:S(2)}) collective-permute-start(f32[8,1,2]{0,2,1:T(2,128)S(1)} %get-tuple-element.52), channel_id=1, source_target_pairs={{0,4},{1,5},{2,6},{3,7},{4,0},{5,1},{6,2},{7,3},{8,12},{9,13},{10,... | collective-permute-start | bytes 200 | tf_op jit(solution)/shard_map/ppermute | solution.py:29
  244.3 7.0 %collective-permute-start.10 = (f32[8,1,2]{0,2,1:T(2,128)S(1)}, f32[8,1,2]{0,2,1:T(2,128)S(1)}, u32[]{:S(2)}, u32[]{:S(2)}) collective-permute-start(f32[8,1,2]{0,2,1:T(2,128)S(1)} %get-tuple-element.51), channel_id=1, source_target_pairs={{0,5},{1,4},{2,7},{3,6},{4,1},{5,0},{6,3},{7,2},{8,13},{9,12},{10,... | collective-permute-start | bytes 200 | tf_op jit(solution)/shard_map/ppermute | solution.py:29
  246.0 5.5 %collective-permute-start.11 = (f32[8,1,2]{0,2,1:T(2,128)S(1)}, f32[8,1,2]{0,2,1:T(2,128)S(1)}, u32[]{:S(2)}, u32[]{:S(2)}) collective-permute-start(f32[8,1,2]{0,2,1:T(2,128)S(1)} %get-tuple-element.50), channel_id=1, source_target_pairs={{0,6},{1,7},{2,4},{3,5},{4,2},{5,3},{6,0},{7,1},{8,14},{9,15},{10,... | collective-permute-start | bytes 200 | tf_op jit(solution)/shard_map/ppermute | solution.py:29
  246.0 8.9 %collective-permute-start.12 = (f32[8,1,2]{0,2,1:T(2,128)S(1)}, f32[8,1,2]{0,2,1:T(2,128)S(1)}, u32[]{:S(2)}, u32[]{:S(2)}) collective-permute-start(f32[8,1,2]{0,2,1:T(2,128)S(1)} %get-tuple-element.49), channel_id=1, source_target_pairs={{0,7},{1,6},{2,5},{3,4},{4,3},{5,2},{6,1},{7,0},{8,15},{9,14},{10,... | collective-permute-start | bytes 200 | tf_op jit(solution)/shard_map/ppermute | solution.py:29
  248.7 6.3 %collective-permute-start.13 = (f32[8,1,2]{0,2,1:T(2,128)S(1)}, f32[8,1,2]{0,2,1:T(2,128)S(1)}, u32[]{:S(2)}, u32[]{:S(2)}) collective-permute-start(f32[8,1,2]{0,2,1:T(2,128)S(1)} %get-tuple-element.48), channel_id=1, source_target_pairs={{0,8},{1,9},{2,10},{3,11},{4,12},{5,13},{6,14},{7,15},{8,0},{9,1},... | collective-permute-start | bytes 200 | tf_op jit(solution)/shard_map/ppermute | solution.py:29
  248.7 9.7 %collective-permute-start.14 = (f32[8,1,2]{0,2,1:T(2,128)S(1)}, f32[8,1,2]{0,2,1:T(2,128)S(1)}, u32[]{:S(2)}, u32[]{:S(2)}) collective-permute-start(f32[8,1,2]{0,2,1:T(2,128)S(1)} %get-tuple-element.47), channel_id=1, source_target_pairs={{0,9},{1,8},{2,11},{3,10},{4,13},{5,12},{6,15},{7,14},{8,1},{9,0},... | collective-permute-start | bytes 200 | tf_op jit(solution)/shard_map/ppermute | solution.py:29
  251.3 7.3 %collective-permute-start.15 = (f32[8,1,2]{0,2,1:T(2,128)S(1)}, f32[8,1,2]{0,2,1:T(2,128)S(1)}, u32[]{:S(2)}, u32[]{:S(2)}) collective-permute-start(f32[8,1,2]{0,2,1:T(2,128)S(1)} %get-tuple-element.46), channel_id=1, source_target_pairs={{0,10},{1,11},{2,8},{3,9},{4,14},{5,15},{6,12},{7,13},{8,2},{9,3},... | collective-permute-start | bytes 200 | tf_op jit(solution)/shard_map/ppermute | solution.py:29
  251.4 11.5 %collective-permute-start.16 = (f32[8,1,2]{0,2,1:T(2,128)S(1)}, f32[8,1,2]{0,2,1:T(2,128)S(1)}, u32[]{:S(2)}, u32[]{:S(2)}) collective-permute-start(f32[8,1,2]{0,2,1:T(2,128)S(1)} %get-tuple-element.45), channel_id=1, source_target_pairs={{0,11},{1,10},{2,9},{3,8},{4,15},{5,14},{6,13},{7,12},{8,3},{9,2},... | collective-permute-start | bytes 200 | tf_op jit(solution)/shard_map/ppermute | solution.py:29
  254.9 8.0 %collective-permute-start.17 = (f32[8,1,2]{0,2,1:T(2,128)S(1)}, f32[8,1,2]{0,2,1:T(2,128)S(1)}, u32[]{:S(2)}, u32[]{:S(2)}) collective-permute-start(f32[8,1,2]{0,2,1:T(2,128)S(1)} %get-tuple-element.44), channel_id=1, source_target_pairs={{0,12},{1,13},{2,14},{3,15},{4,8},{5,9},{6,10},{7,11},{8,4},{9,5},... | collective-permute-start | bytes 200 | tf_op jit(solution)/shard_map/ppermute | solution.py:29
  255.0 8.0 %collective-permute-start.18 = (f32[8,1,2]{0,2,1:T(2,128)S(1)}, f32[8,1,2]{0,2,1:T(2,128)S(1)}, u32[]{:S(2)}, u32[]{:S(2)}) collective-permute-start(f32[8,1,2]{0,2,1:T(2,128)S(1)} %get-tuple-element.43), channel_id=1, source_target_pairs={{0,13},{1,12},{2,15},{3,14},{4,9},{5,8},{6,11},{7,10},{8,5},{9,4},... | collective-permute-start | bytes 200 | tf_op jit(solution)/shard_map/ppermute | solution.py:29
  258.4 6.3 %collective-permute-start.19 = (f32[8,1,2]{0,2,1:T(2,128)S(1)}, f32[8,1,2]{0,2,1:T(2,128)S(1)}, u32[]{:S(2)}, u32[]{:S(2)}) collective-permute-start(f32[8,1,2]{0,2,1:T(2,128)S(1)} %get-tuple-element.42), channel_id=1, source_target_pairs={{0,14},{1,15},{2,12},{3,13},{4,10},{5,11},{6,8},{7,9},{8,6},{9,7},... | collective-permute-start | bytes 200 | tf_op jit(solution)/shard_map/ppermute | solution.py:29
  258.7 6.1 %collective-permute-start.20 = (f32[8,1,2]{0,2,1:T(2,128)S(1)}, f32[8,1,2]{0,2,1:T(2,128)S(1)}, u32[]{:S(2)}, u32[]{:S(2)}) collective-permute-start(f32[8,1,2]{0,2,1:T(2,128)S(1)} %get-tuple-element.41), channel_id=1, source_target_pairs={{0,15},{1,14},{2,13},{3,12},{4,11},{5,10},{6,9},{7,8},{8,7},{9,6},... | collective-permute-start | bytes 200 | tf_op jit(solution)/shard_map/ppermute | solution.py:29
